TPU v7x, 256 devices: a whole 4x4x8 slice. The times are simulated.
256 devices in a mesh: phase: 32 (over z, x_hi, core), gz: 8 (over y, x_lo).
Axes of the slice: x: 4 (x_hi: 2, x_lo: 2; x = x_hi * 2 + x_lo), y: 4, z: 8, core: 2. Of those that a mesh axis runs over, the one named last changes fastest.
Arguments:
- velocity: float32 [32, 3, 512, 16, 128], P('phase', None, 'gz'), may hold values from -3 to 3
- image: float32 [32, 512, 16, 128], P('phase', 'gz'), may hold values from -6 to 6
- target: float32 [32, 512, 16, 128], P('phase', 'gz'), may hold values from -6 to 6
Outputs:
- adjoint: float32 [32, 512, 16, 128], P('phase', 'gz')
- smoothed: float32 [32, 3, 512, 16, 128], P('phase', None, 'gz')
All inputs are finite; a program needn't handle non-finite values.
Results may differ from a plain program's by a relative error of at most 0.00002.
Values sent between devices are 32-bit elements; how exact they have to be, the bound alone decides.
A program may use at most 64 MiB of HBM per device.

v0:
```python
import jax
import jax.numpy as jnp
from jax import lax
from jax.sharding import PartitionSpec as P

STEPS = 4
TAPS = 4


STEP_DT = 0.1
RAW_WEIGHTS = [0.6**order for order in range(5)]
WEIGHT_TOTAL = RAW_WEIGHTS[0] + 2.0 * (
    RAW_WEIGHTS[1] + RAW_WEIGHTS[2] + RAW_WEIGHTS[3] + RAW_WEIGHTS[4]
)
FRAME_WEIGHTS = [value / WEIGHT_TOTAL for value in RAW_WEIGHTS]


def padded(block, sides, width):
    for axis, dim in sides:
        count = lax.axis_size(axis)
        forward = [(i, i + 1) for i in range(count - 1)]
        backward = [(target, source) for source, target in forward]
        low = lax.ppermute(
            lax.slice_in_dim(block, block.shape[dim] - width, None, axis=dim), axis, forward
        )
        high = lax.ppermute(lax.slice_in_dim(block, 0, width, axis=dim), axis, backward)
        block = jnp.concatenate([low, block, high], axis=dim)
    return block


def passed_along(block, axis, distance):
    devices = range(lax.axis_size(axis))
    route = [((i - distance) % len(devices), i) for i in devices]
    return lax.ppermute(block, axis, route)


def window_cut(array, dim, start_at, stop_at):
    selector = [slice(None)] * array.ndim
    for other in range(3):
        place = array.ndim - 3 + other
        if other == dim:
            selector[place] = slice(start_at, stop_at)
        else:
            selector[place] = slice(1, array.shape[place] - 1)
    return array[tuple(selector)]


def transport(padded_field, padded_speed):
    result = window_cut(padded_field, 0, 1, padded_field.shape[0] - 1)
    for dim in range(3):
        extent = padded_field.shape[dim] - 2
        lower_cell = window_cut(padded_field, dim, 0, extent + 1)
        upper_cell = window_cut(padded_field, dim, 1, extent + 2)
        face_speed = 0.5 * (
            window_cut(padded_speed[dim], dim, 0, extent + 1)
            + window_cut(padded_speed[dim], dim, 1, extent + 2)
        )
        face_flux = (
            jnp.maximum(face_speed, 0.0) * lower_cell + jnp.minimum(face_speed, 0.0) * upper_cell
        )
        divergence = lax.slice_in_dim(face_flux, 1, extent + 1, axis=dim) - lax.slice_in_dim(
            face_flux, 0, extent, axis=dim
        )
        result = result - STEP_DT * divergence
    return result


def gradient(padded_image):
    parts = []
    for dim in range(3):
        extent = padded_image.shape[dim] - 2
        parts.append(
            0.5
            * (
                window_cut(padded_image, dim, 2, extent + 2)
                - window_cut(padded_image, dim, 0, extent)
            )
        )
    return jnp.stack(parts)


def local(velocity, image, target):
    source = (image - target)[0]
    own_velocity = velocity[0]
    static = jnp.concatenate([own_velocity, image], axis=0)
    static_ext = padded(static, (("gz", 1),), 1)
    padded_static = jnp.pad(static_ext, ((0, 0), (0, 0), (1, 1), (1, 1)))
    padded_velocity = padded_static[:3]
    padded_image = padded_static[3]
    adjoint = source
    for step in range(STEPS):
        later = passed_along(adjoint, "phase", -1)
        later_ext = padded(later, (("gz", 0),), 1)
        adjoint = source + transport(jnp.pad(later_ext, ((0, 0), (1, 1), (1, 1))), padded_velocity)
    grads = gradient(padded_image)
    descent = own_velocity - adjoint[None] * grads
    smoothed = FRAME_WEIGHTS[0] * descent
    for shift_by in range(1, TAPS + 1):
        ahead = passed_along(descent, "phase", -shift_by)
        behind = passed_along(descent, "phase", shift_by)
        smoothed = smoothed + FRAME_WEIGHTS[shift_by] * (ahead + behind)
    return (adjoint[None], smoothed[None])


def solution(mesh):
    return jax.shard_map(
        local,
        mesh=mesh,
        in_specs=(
            P("phase", None, "gz", None, None),
            P("phase", "gz", None, None),
            P("phase", "gz", None, None),
        ),
        out_specs=(P("phase", "gz", None, None), P("phase", None, "gz", None, None)),
        check_vma=False,
    )
```

profile of v0, /device:TPU:1, one launch (start us, length us, event | category | flops | bytes accessed | tf_op | source)
XLA Modules:
  0.0 246.1 jit_solution(253753512916974801)
XLA Ops:
  1.6 3.9 %collective-permute-start.1 = (f32[4,1,16,128]{3,2,1,0:T(8,128)S(1)}, f32[4,1,16,128]{3,2,1,0:T(8,128)S(1)}, u32[]{:S(2)}, u32[]{:S(2)}) collective-permute-start(f32[4,1,16,128]{3,2,1,0:T(8,128)S(1)} %get-tuple-element.12), channel_id=1, source_target_pairs={{0,1},{1,2},{2,3},{3,4},{4,5},{5,6},{6,7},{8,9},{9,10},{10,11},{11... | collective-permute-start | bytes 98312 | tf_op jit(solution)/shard_map/ppermute | solution.py:23
  5.5 1.3 collective-permute-start.2
  8.0 2.2 collective-permute-done.2
  10.2 4.4 %select_maximum_fusion = f32[4,66,18,130]{3,2,1,0:T(8,128)S(1)} fusion(f32[4,1,16,128]{3,2,1,0:T(8,128)S(1)} %collective-permute-done.2, f32[4,1,16,128]{3,2,1,0:T(8,128)S(1)} %collective-permute-done.1, f32[1,64,16,128]{3,2,1,0:T(8,128)S(1)} %copy-done.2, f32[3,64,16,128]{3,2,1,0:T(8,128)S(1)} %bitcast.24), kind=kLoop, calls=%fused_computation.4 | loop fusion | flops 11119680 | bytes 4633728 | tf_op jit(solution)/shard_map/concatenate | solution.py:27
  14.6 2.5 %collective-permute-done = f32[64,16,128]{2,1,0:T(8,128)S(1)} collective-permute-done((f32[64,16,128]{2,1,0:T(8,128)S(1)}, f32[64,16,128]{2,1,0:T(8,128)S(1)}, u32[]{:S(2)}, u32[]{:S(2)}) %collective-permute-start) | collective-permute-done | bytes 524320 | tf_op jit(solution)/shard_map/ppermute | solution.py:34
  17.2 3.9 %collective-permute-start.3 = (f32[1,16,128]{2,1,0:T(8,128)S(1)}, f32[1,16,128]{2,1,0:T(8,128)S(1)}, u32[]{:S(2)}, u32[]{:S(2)}) collective-permute-start(f32[1,16,128]{2,1,0:T(8,128)S(1)} %get-tuple-element.23), channel_id=1, source_target_pairs={{0,1},{1,2},{2,3},{3,4},{4,5},{5,6},{6,7},{8,9},{9,10},{10,11},{11... | collective-permute-start | bytes 24584 | tf_op jit(solution)/shard_map/ppermute | solution.py:23
  21.1 1.3 collective-permute-start.4
  22.8 4.1 %collective-permute-done.4 = f32[1,16,128]{2,1,0:T(8,128)S(1)} collective-permute-done((f32[1,16,128]{2,1,0:T(8,128)S(1)}, f32[1,16,128]{2,1,0:T(8,128)S(1)}, u32[]{:S(2)}, u32[]{:S(2)}) %collective-permute-start.4) | collective-permute-done | bytes 8224 | tf_op jit(solution)/shard_map/ppermute | solution.py:26
  29.9 5.5 %collective-permute-start.5 = (f32[64,16,128]{2,1,0:T(8,128)S(1)}, f32[64,16,128]{2,1,0:T(8,128)S(1)}, u32[]{:S(2)}, u32[]{:S(2)}) collective-permute-start(f32[64,16,128]{2,1,0:T(8,128)S(1)} %fusion.51), channel_id=1, source_target_pairs={{8,0},{16,8},{24,16},{32,24},{40,32},{48,40},{56,48},{64,56},{72,6... | collective-permute-start | bytes 1572872 | tf_op jit(solution)/shard_map/ppermute | solution.py:34
  35.4 4.7 %collective-permute-done.5 = f32[64,16,128]{2,1,0:T(8,128)S(1)} collective-permute-done((f32[64,16,128]{2,1,0:T(8,128)S(1)}, f32[64,16,128]{2,1,0:T(8,128)S(1)}, u32[]{:S(2)}, u32[]{:S(2)}) %collective-permute-start.5) | collective-permute-done | bytes 524320 | tf_op jit(solution)/shard_map/ppermute | solution.py:34
  40.1 4.2 %collective-permute-start.6 = (f32[1,16,128]{2,1,0:T(8,128)S(1)}, f32[1,16,128]{2,1,0:T(8,128)S(1)}, u32[]{:S(2)}, u32[]{:S(2)}) collective-permute-start(f32[1,16,128]{2,1,0:T(8,128)S(1)} %get-tuple-element.21), channel_id=1, source_target_pairs={{0,1},{1,2},{2,3},{3,4},{4,5},{5,6},{6,7},{8,9},{9,10},{10,11},{11... | collective-permute-start | bytes 24584 | tf_op jit(solution)/shard_map/ppermute | solution.py:23
  44.4 1.3 collective-permute-start.7
  45.7 3.1 %collective-permute-done.7 = f32[1,16,128]{2,1,0:T(8,128)S(1)} collective-permute-done((f32[1,16,128]{2,1,0:T(8,128)S(1)}, f32[1,16,128]{2,1,0:T(8,128)S(1)}, u32[]{:S(2)}, u32[]{:S(2)}) %collective-permute-start.7) | collective-permute-done | bytes 8224 | tf_op jit(solution)/shard_map/ppermute | solution.py:26
  50.6 7.3 %collective-permute-start.8 = (f32[64,16,128]{2,1,0:T(8,128)S(1)}, f32[64,16,128]{2,1,0:T(8,128)S(1)}, u32[]{:S(2)}, u32[]{:S(2)}) collective-permute-start(f32[64,16,128]{2,1,0:T(8,128)S(1)} %fusion.44), channel_id=1, source_target_pairs={{8,0},{16,8},{24,16},{32,24},{40,32},{48,40},{56,48},{64,56},{72,6... | collective-permute-start | bytes 1572872 | tf_op jit(solution)/shard_map/ppermute | solution.py:34
  57.8 2.9 %collective-permute-done.8 = f32[64,16,128]{2,1,0:T(8,128)S(1)} collective-permute-done((f32[64,16,128]{2,1,0:T(8,128)S(1)}, f32[64,16,128]{2,1,0:T(8,128)S(1)}, u32[]{:S(2)}, u32[]{:S(2)}) %collective-permute-start.8) | collective-permute-done | bytes 524320 | tf_op jit(solution)/shard_map/ppermute | solution.py:34
  60.8 2.9 %collective-permute-start.9 = (f32[1,16,128]{2,1,0:T(8,128)S(1)}, f32[1,16,128]{2,1,0:T(8,128)S(1)}, u32[]{:S(2)}, u32[]{:S(2)}) collective-permute-start(f32[1,16,128]{2,1,0:T(8,128)S(1)} %get-tuple-element.19), channel_id=1, source_target_pairs={{0,1},{1,2},{2,3},{3,4},{4,5},{5,6},{6,7},{8,9},{9,10},{10,11},{11... | collective-permute-start | bytes 24584 | tf_op jit(solution)/shard_map/ppermute | solution.py:23
  65.0 3.1 %collective-permute-done.10 = f32[1,16,128]{2,1,0:T(8,128)S(1)} collective-permute-done((f32[1,16,128]{2,1,0:T(8,128)S(1)}, f32[1,16,128]{2,1,0:T(8,128)S(1)}, u32[]{:S(2)}, u32[]{:S(2)}) %collective-permute-start.10) | collective-permute-done | bytes 8224 | tf_op jit(solution)/shard_map/ppermute | solution.py:26
  69.9 9.9 %collective-permute-start.11 = (f32[64,16,128]{2,1,0:T(8,128)S(1)}, f32[64,16,128]{2,1,0:T(8,128)S(1)}, u32[]{:S(2)}, u32[]{:S(2)}) collective-permute-start(f32[64,16,128]{2,1,0:T(8,128)S(1)} %fusion.37), channel_id=1, source_target_pairs={{8,0},{16,8},{24,16},{32,24},{40,32},{48,40},{56,48},{64,56},{72,6... | collective-permute-start | bytes 1572872 | tf_op jit(solution)/shard_map/ppermute | solution.py:34
  79.8 1.5 collective-permute-done.11
  81.3 4.5 %collective-permute-start.12 = (f32[1,16,128]{2,1,0:T(8,128)S(1)}, f32[1,16,128]{2,1,0:T(8,128)S(1)}, u32[]{:S(2)}, u32[]{:S(2)}) collective-permute-start(f32[1,16,128]{2,1,0:T(8,128)S(1)} %get-tuple-element.17), channel_id=1, source_target_pairs={{0,1},{1,2},{2,3},{3,4},{4,5},{5,6},{6,7},{8,9},{9,10},{10,11},{11... | collective-permute-start | bytes 24584 | tf_op jit(solution)/shard_map/ppermute | solution.py:23
  87.9 2.3 collective-permute-done.13
  92.4 5.3 %collective-permute-start.20 = (f32[3,64,16,128]{3,2,1,0:T(8,128)S(1)}, f32[3,64,16,128]{3,2,1,0:T(8,128)S(1)}, u32[]{:S(2)}, u32[]{:S(2)}) collective-permute-start(f32[3,64,16,128]{3,2,1,0:T(8,128)S(1)} %fusion.6), channel_id=1, source_target_pairs={{32,0},{40,8},{48,16},{56,24},{64,32},{72,40},{80,48},{88,56},{96,... | collective-permute-start | bytes 4718600 | tf_op jit(solution)/shard_map/ppermute | solution.py:34
  97.7 6.7 %collective-permute-start.19 = (f32[3,64,16,128]{3,2,1,0:T(8,128)S(1)}, f32[3,64,16,128]{3,2,1,0:T(8,128)S(1)}, u32[]{:S(2)}, u32[]{:S(2)}) collective-permute-start(f32[3,64,16,128]{3,2,1,0:T(8,128)S(1)} %fusion.6), channel_id=1, source_target_pairs={{232,0},{240,8},{248,16},{0,24},{8,32},{16,40},{24,48},{32,56},{40... | collective-permute-start | bytes 4718600 | tf_op jit(solution)/shard_map/ppermute | solution.py:34
  104.4 6.9 %collective-permute-start.17 = (f32[3,64,16,128]{3,2,1,0:T(8,128)S(1)}, f32[3,64,16,128]{3,2,1,0:T(8,128)S(1)}, u32[]{:S(2)}, u32[]{:S(2)}) collective-permute-start(f32[3,64,16,128]{3,2,1,0:T(8,128)S(1)} %fusion.6), channel_id=1, source_target_pairs={{240,0},{248,8},{0,16},{8,24},{16,32},{24,40},{32,48},{40,56},{48,... | collective-permute-start | bytes 4718600 | tf_op jit(solution)/shard_map/ppermute | solution.py:34
  111.3 15.4 %collective-permute-done.20 = f32[3,64,16,128]{3,2,1,0:T(8,128)S(1)} collective-permute-done((f32[3,64,16,128]{3,2,1,0:T(8,128)S(1)}, f32[3,64,16,128]{3,2,1,0:T(8,128)S(1)}, u32[]{:S(2)}, u32[]{:S(2)}) %collective-permute-start.20) | collective-permute-done | bytes 1572896 | tf_op jit(solution)/shard_map/ppermute | solution.py:34
  127.0 6.6 %collective-permute-done.19 = f32[3,64,16,128]{3,2,1,0:T(8,128)S(1)} collective-permute-done((f32[3,64,16,128]{3,2,1,0:T(8,128)S(1)}, f32[3,64,16,128]{3,2,1,0:T(8,128)S(1)}, u32[]{:S(2)}, u32[]{:S(2)}) %collective-permute-start.19) | collective-permute-done | bytes 1572896 | tf_op jit(solution)/shard_map/ppermute | solution.py:34
  133.5 29.5 %collective-permute-start.14 = (f32[3,64,16,128]{3,2,1,0:T(8,128)S(1)}, f32[3,64,16,128]{3,2,1,0:T(8,128)S(1)}, u32[]{:S(2)}, u32[]{:S(2)}) collective-permute-start(f32[3,64,16,128]{3,2,1,0:T(8,128)S(1)} %fusion.6), channel_id=1, source_target_pairs={{8,0},{16,8},{24,16},{32,24},{40,32},{48,40},{56,48},{64,56},{72,6... | collective-permute-start | bytes 4718600 | tf_op jit(solution)/shard_map/ppermute | solution.py:34
  163.0 10.3 %collective-permute-done.18 = f32[3,64,16,128]{3,2,1,0:T(8,128)S(1)} collective-permute-done((f32[3,64,16,128]{3,2,1,0:T(8,128)S(1)}, f32[3,64,16,128]{3,2,1,0:T(8,128)S(1)}, u32[]{:S(2)}, u32[]{:S(2)}) %collective-permute-start.18) | collective-permute-done | bytes 1572896 | tf_op jit(solution)/shard_map/ppermute | solution.py:34
  173.3 39.4 %collective-permute-done.17 = f32[3,64,16,128]{3,2,1,0:T(8,128)S(1)} collective-permute-done((f32[3,64,16,128]{3,2,1,0:T(8,128)S(1)}, f32[3,64,16,128]{3,2,1,0:T(8,128)S(1)}, u32[]{:S(2)}, u32[]{:S(2)}) %collective-permute-start.17) | collective-permute-done | bytes 1572896 | tf_op jit(solution)/shard_map/ppermute | solution.py:34
  212.7 27.6 %collective-permute-done.16 = f32[3,64,16,128]{3,2,1,0:T(8,128)S(1)} collective-permute-done((f32[3,64,16,128]{3,2,1,0:T(8,128)S(1)}, f32[3,64,16,128]{3,2,1,0:T(8,128)S(1)}, u32[]{:S(2)}, u32[]{:S(2)}) %collective-permute-start.16) | collective-permute-done | bytes 1572896 | tf_op jit(solution)/shard_map/ppermute | solution.py:34
  240.3 3.6 %collective-permute-done.15 = f32[3,64,16,128]{3,2,1,0:T(8,128)S(1)} collective-permute-done((f32[3,64,16,128]{3,2,1,0:T(8,128)S(1)}, f32[3,64,16,128]{3,2,1,0:T(8,128)S(1)}, u32[]{:S(2)}, u32[]{:S(2)}) %collective-permute-start.15) | collective-permute-done | bytes 1572896 | tf_op jit(solution)/shard_map/ppermute | solution.py:34
  243.9 2.2 add_bitcast_fusion
  (51 shorter events, 14.7 us)
Async XLA Ops:
  0.6 6.2 %copy-start.2 = (f32[1,64,16,128]{3,2,1,0:T(8,128)S(1)}, f32[1,64,16,128]{3,2,1,0:T(8,128)}, u32[]{:S(2)}) copy-start(f32[1,64,16,128]{3,2,1,0:T(8,128)} %param.4) | copy-start | bytes 1572868
  0.6 6.2 %copy-start.3 = (f32[1,64,16,128]{3,2,1,0:T(8,128)S(1)}, f32[1,64,16,128]{3,2,1,0:T(8,128)}, u32[]{:S(2)}) copy-start(f32[1,64,16,128]{3,2,1,0:T(8,128)} %param.5) | copy-start | bytes 1572868
  0.6 9.5 %copy-start = (f32[1,3,64,16,128]{4,3,2,1,0:T(8,128)S(1)}, f32[1,3,64,16,128]{4,3,2,1,0:T(8,128)}, u32[]{:S(2)}) copy-start(f32[1,3,64,16,128]{4,3,2,1,0:T(8,128)} %param.3) | copy-start | bytes 4718596
  1.6 6.4 %collective-permute-start.1 = (f32[4,1,16,128]{3,2,1,0:T(8,128)S(1)}, f32[4,1,16,128]{3,2,1,0:T(8,128)S(1)}, u32[]{:S(2)}, u32[]{:S(2)}) collective-permute-start(f32[4,1,16,128]{3,2,1,0:T(8,128)S(1)} %get-tuple-element.12), channel_id=1, source_target_pairs={{0,1},{1,2},{2,3},{3,4},{4,5},{5,6},{6,7},{8,9},{9,10},{10,11},{11... | collective-permute-start | bytes 98312 | tf_op jit(solution)/shard_map/ppermute | solution.py:23
  5.5 4.7 %collective-permute-start.2 = (f32[4,1,16,128]{3,2,1,0:T(8,128)S(1)}, f32[4,1,16,128]{3,2,1,0:T(8,128)S(1)}, u32[]{:S(2)}, u32[]{:S(2)}) collective-permute-start(f32[4,1,16,128]{3,2,1,0:T(8,128)S(1)} %get-tuple-element.13), channel_id=1, source_target_pairs={{1,0},{2,1},{3,2},{4,3},{5,4},{6,5},{7,6},{9,8},{10,9},{11,10},{12... | collective-permute-start | bytes 98312 | tf_op jit(solution)/shard_map/ppermute | solution.py:26
  6.9 10.2 %collective-permute-start = (f32[64,16,128]{2,1,0:T(8,128)S(1)}, f32[64,16,128]{2,1,0:T(8,128)S(1)}, u32[]{:S(2)}, u32[]{:S(2)}) collective-permute-start(f32[64,16,128]{2,1,0:T(8,128)S(1)} %subtract_bitcast_fusion), channel_id=1, source_target_pairs={{8,0},{16,8},{24,16},{32,24},{40,32},{48,40},{56,48},{64,56},{72,6... | collective-permute-start | bytes 1572872 | tf_op jit(solution)/shard_map/ppermute | solution.py:34
  17.2 5.7 %collective-permute-start.3 = (f32[1,16,128]{2,1,0:T(8,128)S(1)}, f32[1,16,128]{2,1,0:T(8,128)S(1)}, u32[]{:S(2)}, u32[]{:S(2)}) collective-permute-start(f32[1,16,128]{2,1,0:T(8,128)S(1)} %get-tuple-element.23), channel_id=1, source_target_pairs={{0,1},{1,2},{2,3},{3,4},{4,5},{5,6},{6,7},{8,9},{9,10},{10,11},{11... | collective-permute-start | bytes 24584 | tf_op jit(solution)/shard_map/ppermute | solution.py:23
  21.1 5.9 %collective-permute-start.4 = (f32[1,16,128]{2,1,0:T(8,128)S(1)}, f32[1,16,128]{2,1,0:T(8,128)S(1)}, u32[]{:S(2)}, u32[]{:S(2)}) collective-permute-start(f32[1,16,128]{2,1,0:T(8,128)S(1)} %get-tuple-element.24), channel_id=1, source_target_pairs={{1,0},{2,1},{3,2},{4,3},{5,4},{6,5},{7,6},{9,8},{10,9},{11,10},{12... | collective-permute-start | bytes 24584 | tf_op jit(solution)/shard_map/ppermute | solution.py:26
  29.9 10.2 %collective-permute-start.5 = (f32[64,16,128]{2,1,0:T(8,128)S(1)}, f32[64,16,128]{2,1,0:T(8,128)S(1)}, u32[]{:S(2)}, u32[]{:S(2)}) collective-permute-start(f32[64,16,128]{2,1,0:T(8,128)S(1)} %fusion.51), channel_id=1, source_target_pairs={{8,0},{16,8},{24,16},{32,24},{40,32},{48,40},{56,48},{64,56},{72,6... | collective-permute-start | bytes 1572872 | tf_op jit(solution)/shard_map/ppermute | solution.py:34
  40.1 5.6 %collective-permute-start.6 = (f32[1,16,128]{2,1,0:T(8,128)S(1)}, f32[1,16,128]{2,1,0:T(8,128)S(1)}, u32[]{:S(2)}, u32[]{:S(2)}) collective-permute-start(f32[1,16,128]{2,1,0:T(8,128)S(1)} %get-tuple-element.21), channel_id=1, source_target_pairs={{0,1},{1,2},{2,3},{3,4},{4,5},{5,6},{6,7},{8,9},{9,10},{10,11},{11... | collective-permute-start | bytes 24584 | tf_op jit(solution)/shard_map/ppermute | solution.py:23
  44.4 4.4 %collective-permute-start.7 = (f32[1,16,128]{2,1,0:T(8,128)S(1)}, f32[1,16,128]{2,1,0:T(8,128)S(1)}, u32[]{:S(2)}, u32[]{:S(2)}) collective-permute-start(f32[1,16,128]{2,1,0:T(8,128)S(1)} %get-tuple-element.22), channel_id=1, source_target_pairs={{1,0},{2,1},{3,2},{4,3},{5,4},{6,5},{7,6},{9,8},{10,9},{11,10},{12... | collective-permute-start | bytes 24584 | tf_op jit(solution)/shard_map/ppermute | solution.py:26
  50.6 10.2 %collective-permute-start.8 = (f32[64,16,128]{2,1,0:T(8,128)S(1)}, f32[64,16,128]{2,1,0:T(8,128)S(1)}, u32[]{:S(2)}, u32[]{:S(2)}) collective-permute-start(f32[64,16,128]{2,1,0:T(8,128)S(1)} %fusion.44), channel_id=1, source_target_pairs={{8,0},{16,8},{24,16},{32,24},{40,32},{48,40},{56,48},{64,56},{72,6... | collective-permute-start | bytes 1572872 | tf_op jit(solution)/shard_map/ppermute | solution.py:34
  60.8 4.2 %collective-permute-start.9 = (f32[1,16,128]{2,1,0:T(8,128)S(1)}, f32[1,16,128]{2,1,0:T(8,128)S(1)}, u32[]{:S(2)}, u32[]{:S(2)}) collective-permute-start(f32[1,16,128]{2,1,0:T(8,128)S(1)} %get-tuple-element.19), channel_id=1, source_target_pairs={{0,1},{1,2},{2,3},{3,4},{4,5},{5,6},{6,7},{8,9},{9,10},{10,11},{11... | collective-permute-start | bytes 24584 | tf_op jit(solution)/shard_map/ppermute | solution.py:23
  63.7 4.4 %collective-permute-start.10 = (f32[1,16,128]{2,1,0:T(8,128)S(1)}, f32[1,16,128]{2,1,0:T(8,128)S(1)}, u32[]{:S(2)}, u32[]{:S(2)}) collective-permute-start(f32[1,16,128]{2,1,0:T(8,128)S(1)} %get-tuple-element.20), channel_id=1, source_target_pairs={{1,0},{2,1},{3,2},{4,3},{5,4},{6,5},{7,6},{9,8},{10,9},{11,10},{12... | collective-permute-start | bytes 24584 | tf_op jit(solution)/shard_map/ppermute | solution.py:26
  69.9 11.4 %collective-permute-start.11 = (f32[64,16,128]{2,1,0:T(8,128)S(1)}, f32[64,16,128]{2,1,0:T(8,128)S(1)}, u32[]{:S(2)}, u32[]{:S(2)}) collective-permute-start(f32[64,16,128]{2,1,0:T(8,128)S(1)} %fusion.37), channel_id=1, source_target_pairs={{8,0},{16,8},{24,16},{32,24},{40,32},{48,40},{56,48},{64,56},{72,6... | collective-permute-start | bytes 1572872 | tf_op jit(solution)/shard_map/ppermute | solution.py:34
  81.3 6.6 %collective-permute-start.12 = (f32[1,16,128]{2,1,0:T(8,128)S(1)}, f32[1,16,128]{2,1,0:T(8,128)S(1)}, u32[]{:S(2)}, u32[]{:S(2)}) collective-permute-start(f32[1,16,128]{2,1,0:T(8,128)S(1)} %get-tuple-element.17), channel_id=1, source_target_pairs={{0,1},{1,2},{2,3},{3,4},{4,5},{5,6},{6,7},{8,9},{9,10},{10,11},{11... | collective-permute-start | bytes 24584 | tf_op jit(solution)/shard_map/ppermute | solution.py:23
  85.9 4.4 %collective-permute-start.13 = (f32[1,16,128]{2,1,0:T(8,128)S(1)}, f32[1,16,128]{2,1,0:T(8,128)S(1)}, u32[]{:S(2)}, u32[]{:S(2)}) collective-permute-start(f32[1,16,128]{2,1,0:T(8,128)S(1)} %get-tuple-element.18), channel_id=1, source_target_pairs={{1,0},{2,1},{3,2},{4,3},{5,4},{6,5},{7,6},{9,8},{10,9},{11,10},{12... | collective-permute-start | bytes 24584 | tf_op jit(solution)/shard_map/ppermute | solution.py:26
  92.1 151.8 %copy-start.1 = (f32[64,16,128]{2,1,0:T(8,128)}, f32[64,16,128]{2,1,0:T(8,128)S(1)}, u32[]{:S(2)}) copy-start(f32[64,16,128]{2,1,0:T(8,128)S(1)} %fusion.30) | copy-start | bytes 1572868
  92.4 34.3 %collective-permute-start.20 = (f32[3,64,16,128]{3,2,1,0:T(8,128)S(1)}, f32[3,64,16,128]{3,2,1,0:T(8,128)S(1)}, u32[]{:S(2)}, u32[]{:S(2)}) collective-permute-start(f32[3,64,16,128]{3,2,1,0:T(8,128)S(1)} %fusion.6), channel_id=1, source_target_pairs={{32,0},{40,8},{48,16},{56,24},{64,32},{72,40},{80,48},{88,56},{96,... | collective-permute-start | bytes 4718600 | tf_op jit(solution)/shard_map/ppermute | solution.py:34
  97.7 35.8 %collective-permute-start.19 = (f32[3,64,16,128]{3,2,1,0:T(8,128)S(1)}, f32[3,64,16,128]{3,2,1,0:T(8,128)S(1)}, u32[]{:S(2)}, u32[]{:S(2)}) collective-permute-start(f32[3,64,16,128]{3,2,1,0:T(8,128)S(1)} %fusion.6), channel_id=1, source_target_pairs={{232,0},{240,8},{248,16},{0,24},{8,32},{16,40},{24,48},{32,56},{40... | collective-permute-start | bytes 4718600 | tf_op jit(solution)/shard_map/ppermute | solution.py:34
  104.4 68.9 %collective-permute-start.18 = (f32[3,64,16,128]{3,2,1,0:T(8,128)S(1)}, f32[3,64,16,128]{3,2,1,0:T(8,128)S(1)}, u32[]{:S(2)}, u32[]{:S(2)}) collective-permute-start(f32[3,64,16,128]{3,2,1,0:T(8,128)S(1)} %fusion.6), channel_id=1, source_target_pairs={{24,0},{32,8},{40,16},{48,24},{56,32},{64,40},{72,48},{80,56},{88,... | collective-permute-start | bytes 4718600 | tf_op jit(solution)/shard_map/ppermute | solution.py:34
  104.4 108.3 %collective-permute-start.17 = (f32[3,64,16,128]{3,2,1,0:T(8,128)S(1)}, f32[3,64,16,128]{3,2,1,0:T(8,128)S(1)}, u32[]{:S(2)}, u32[]{:S(2)}) collective-permute-start(f32[3,64,16,128]{3,2,1,0:T(8,128)S(1)} %fusion.6), channel_id=1, source_target_pairs={{240,0},{248,8},{0,16},{8,24},{16,32},{24,40},{32,48},{40,56},{48,... | collective-permute-start | bytes 4718600 | tf_op jit(solution)/shard_map/ppermute | solution.py:34
  111.2 129.1 %collective-permute-start.16 = (f32[3,64,16,128]{3,2,1,0:T(8,128)S(1)}, f32[3,64,16,128]{3,2,1,0:T(8,128)S(1)}, u32[]{:S(2)}, u32[]{:S(2)}) collective-permute-start(f32[3,64,16,128]{3,2,1,0:T(8,128)S(1)} %fusion.6), channel_id=1, source_target_pairs={{16,0},{24,8},{32,16},{40,24},{48,32},{56,40},{64,48},{72,56},{80,... | collective-permute-start | bytes 4718600 | tf_op jit(solution)/shard_map/ppermute | solution.py:34
  126.7 117.2 %collective-permute-start.15 = (f32[3,64,16,128]{3,2,1,0:T(8,128)S(1)}, f32[3,64,16,128]{3,2,1,0:T(8,128)S(1)}, u32[]{:S(2)}, u32[]{:S(2)}) collective-permute-start(f32[3,64,16,128]{3,2,1,0:T(8,128)S(1)} %fusion.6), channel_id=1, source_target_pairs={{248,0},{0,8},{8,16},{16,24},{24,32},{32,40},{40,48},{48,56},{56,6... | collective-permute-start | bytes 4718600 | tf_op jit(solution)/shard_map/ppermute | solution.py:34
  133.5 110.4 %collective-permute-start.14 = (f32[3,64,16,128]{3,2,1,0:T(8,128)S(1)}, f32[3,64,16,128]{3,2,1,0:T(8,128)S(1)}, u32[]{:S(2)}, u32[]{:S(2)}) collective-permute-start(f32[3,64,16,128]{3,2,1,0:T(8,128)S(1)} %fusion.6), channel_id=1, source_target_pairs={{8,0},{16,8},{24,16},{32,24},{40,32},{48,40},{56,48},{64,56},{72,6... | collective-permute-start | bytes 4718600 | tf_op jit(solution)/shard_map/ppermute | solution.py:34
  173.3 70.6 %collective-permute-start.21 = (f32[3,64,16,128]{3,2,1,0:T(8,128)S(1)}, f32[3,64,16,128]{3,2,1,0:T(8,128)S(1)}, u32[]{:S(2)}, u32[]{:S(2)}) collective-permute-start(f32[3,64,16,128]{3,2,1,0:T(8,128)S(1)} %fusion.6), channel_id=1, source_target_pairs={{224,0},{232,8},{240,16},{248,24},{0,32},{8,40},{16,48},{24,56},{3... | collective-permute-start | bytes 4718600 | tf_op jit(solution)/shard_map/ppermute | solution.py:34
where the time goes:
time: 247 us; the launch traced here: 246 us
  waiting for transfers between devices  129 us (52%)
  starting transfers between devices  98.3 us (40%)
  other arithmetic  16.9 us (7%)
    ppermute x12, waiting for transfers between devices, passed_along(): return lax.ppermute(block, axis, route)  115 us
    ppermute x12, starting transfers between devices, passed_along(): return lax.ppermute(block, axis, route)  72.3 us
    ppermute x5, starting transfers between devices, padded(): lax.ppermute(lax.slice_in_dim(block, block.shape[dim] - width, None, axis...  19.6 us
    ppermute x5, waiting for transfers between devices, padded(): lax.ppermute(lax.slice_in_dim(block, 0, width, axis=dim), axis, backward)  14.9 us
    ppermute x5, starting transfers between devices, padded(): lax.ppermute(lax.slice_in_dim(block, 0, width, axis=dim), axis, backward)  6.46 us
    concatenate x5, other arithmetic, padded(): block = jnp.concatenate([low, block, high], axis=dim)  6.36 us
    add x12, other arithmetic, transport(): jnp.maximum(face_speed, 0.0) * lower_cell  5.13 us
  transfers between devices with their start and end apart: 22, of which 15 were waited for; matrix products, arithmetic and copies ran while one was open for 2% of the time, Pallas kernels for 0%

commit v1 on v0

v1 whole, which is shorter than its diff:
```python
import functools

import jax
import jax.numpy as jnp
from jax import lax
from jax.experimental import pallas as pl
from jax.experimental.pallas import tpu as pltpu
from jax.sharding import PartitionSpec as P

MESH = pl.DeviceIdType.MESH
STEPS = 4
TAPS = 4
STEP_DT = 0.1
RAW_WEIGHTS = [0.6**order for order in range(5)]
WEIGHT_TOTAL = RAW_WEIGHTS[0] + 2.0 * (
    RAW_WEIGHTS[1] + RAW_WEIGHTS[2] + RAW_WEIGHTS[3] + RAW_WEIGHTS[4]
)
FRAME_WEIGHTS = [value / WEIGHT_TOTAL for value in RAW_WEIGHTS]

GROUP = 4
QP = 16
XW, YW = 16, 128
HALVES = 2
CP = QP // HALVES


def flip(g):
    return g + 1 - 2 * lax.rem(g, 2)


def kernel(
    phases,
    slabs,
    v_ref,
    img_ref,
    tgt_ref,
    adj_out,
    smo_out,
    img_own,
    tgt_own,
    s_own,
    v0,
    v12,
    img,
    lam,
    lam_in,
    coef,
    adj,
    des,
    des_far,
    smo,
    load_sem,
    in_send,
    in_recv,
    edge_send,
    edge_recv,
    lz_send,
    lz_recv,
    adj_send,
    adj_recv,
    d_send,
    d_recv,
    o_send,
    o_recv,
):
    phase = lax.axis_index("phase")
    slab = lax.axis_index("gz")
    q = lax.rem(phase, GROUP)
    base = phase - q
    upper_base = lax.rem(base + GROUP, phases)
    lower_base = lax.rem(base + phases - GROUP, phases)
    other = flip(slab)
    quarters = slabs * GROUP
    place = other * GROUP + q
    after = lax.rem(place + 1, quarters)
    before = lax.rem(place + quarters - 1, quarters)
    after_q, after_slab = lax.rem(after, GROUP), flip(lax.div(after, GROUP))
    before_q, before_slab = lax.rem(before, GROUP), flip(lax.div(before, GROUP))
    not_first = jnp.where(place == 0, 0.0, 1.0)
    not_last = jnp.where(place == quarters - 1, 0.0, 1.0)

    started = []

    def send(src, dst, send_sem, recv_sem, device):
        copy = pltpu.make_async_remote_copy(
            src_ref=src,
            dst_ref=dst,
            send_sem=send_sem,
            recv_sem=recv_sem,
            device_id=device,
            device_id_type=MESH,
        )
        copy.start()
        started.append(copy)

    def arrived(dst, send_sem, recv_sem):
        pltpu.make_async_remote_copy(
            src_ref=dst,
            dst_ref=dst,
            send_sem=send_sem,
            recv_sem=recv_sem,
            device_id=(phase, slab),
            device_id_type=MESH,
        ).wait_recv()

    loads = [
        pltpu.make_async_copy(img_ref.at[0], img_own, load_sem.at[0]),
        pltpu.make_async_copy(tgt_ref.at[0], tgt_own, load_sem.at[1]),
    ]
    for load in loads:
        load.start()

    partners = [(base + j, other) for j in range(GROUP)]
    partners += [(upper_base + q, slab), (lower_base + q, slab)]
    for here in (base, upper_base, lower_base):
        partners += [(here + after_q, after_slab), (here + before_q, before_slab)]
    barrier = pltpu.get_barrier_semaphore()
    for partner in partners:
        pl.semaphore_signal(barrier, inc=1, device_id=partner, device_id_type=MESH)
    pl.semaphore_wait(barrier, len(partners))

    def scatter(field, source, dest):
        for j in range(GROUP):
            send(
                source(j),
                dest,
                in_send.at[field, j],
                in_recv.at[field, q],
                (base + j, other),
            )

    def gathered(field, dest):
        for i in range(GROUP):
            arrived(dest(i), in_send.at[field, i], in_recv.at[field, i])

    inner = pl.ds(1, QP)
    scatter(0, lambda j: v_ref.at[0, 0, pl.ds(QP * j, QP)], v0.at[q, inner])
    for load in loads:
        load.wait()

    @pl.loop(0, QP)
    def _(t):
        for r in range(GROUP):
            s_own[t * GROUP + r] = img_own[t * GROUP + r] - tgt_own[t * GROUP + r]

    scatter(1, lambda j: s_own.at[pl.ds(QP * j, QP)], lam.at[0, q, inner])
    scatter(2, lambda j: v_ref.at[0, pl.ds(1, 2), pl.ds(QP * j, QP)], v12.at[q])
    scatter(3, lambda j: img_ref.at[0, pl.ds(QP * j, QP)], img.at[q, inner])

    def send_edges(slot, buffer, dest, here):
        send(
            buffer(1),
            dest(QP + 1),
            edge_send.at[slot, 0],
            edge_recv.at[slot, 0],
            (here + before_q, before_slab),
        )
        send(
            buffer(QP),
            dest(0),
            edge_send.at[slot, 1],
            edge_recv.at[slot, 1],
            (here + after_q, after_slab),
        )

    def edges_arrived(slot, dest):
        arrived(dest(QP + 1), edge_send.at[slot, 0], edge_recv.at[slot, 0])
        arrived(dest(0), edge_send.at[slot, 1], edge_recv.at[slot, 1])

    def send_first(k):
        send(
            lam.at[k, 0, inner],
            lam_in.at[k, inner],
            lz_send.at[k],
            lz_recv.at[k],
            (lower_base + q, slab),
        )
        send_edges(
            2 * k,
            lambda plane: lam.at[k, 0, plane],
            lambda plane: lam_in.at[k, plane],
            lower_base,
        )

    def first_arrived(k):
        arrived(lam_in.at[k, inner], lz_send.at[k], lz_recv.at[k])
        edges_arrived(2 * k, lambda plane: lam_in.at[k, plane])

    def rest_edges(k):
        return lambda plane: lam.at[k, pl.ds(1, GROUP - 1), plane]

    def send_rest(k):
        send_edges(2 * k + 1, rest_edges(k), rest_edges(k), base)

    v0_edges = lambda plane: v0.at[:, plane]
    img_edges = lambda plane: img.at[:, plane]
    V_SLOT, IMG_SLOT = 2 * STEPS, 2 * STEPS + 1

    gathered(0, lambda i: v0.at[i, inner])
    send_edges(V_SLOT, v0_edges, v0_edges, base)
    gathered(1, lambda i: lam.at[0, i, inner])
    send_first(0)
    send_rest(0)
    edges_arrived(V_SLOT, v0_edges)
    gathered(2, lambda i: v12.at[i])

    row = lax.broadcasted_iota(jnp.int32, (XW, YW), 0)
    lane = lax.broadcasted_iota(jnp.int32, (XW, YW), 1)

    def shifted(a, axis):
        size = (XW, YW)[axis]
        return pltpu.roll(a, 1, axis), pltpu.roll(a, size - 1, axis)

    dt = STEP_DT
    at_low = (row == 0, lane == 0)
    at_high = (row == XW - 1, lane == YW - 1)

    @pl.loop(0, QP)
    def _(t):
        keep_low = jnp.where(t == 0, not_first, 1.0)
        keep_high = jnp.where(t == QP - 1, not_last, 1.0)
        for i in range(GROUP):
            mid = v0[i, t + 1]
            w_low = 0.5 * (v0[i, t] * keep_low + mid)
            w_high = 0.5 * (v0[i, t + 2] * keep_high + mid)
            total = jnp.maximum(w_high, 0.0) - jnp.minimum(w_low, 0.0)
            coef[i, t, 1] = (dt * keep_low) * jnp.maximum(w_low, 0.0)
            coef[i, t, 2] = (-dt * keep_high) * jnp.minimum(w_high, 0.0)
            for axis in range(2):
                mid = v12[i, axis, t]
                low, high = shifted(mid, axis)
                w_low = 0.5 * (jnp.where(at_low[axis], 0.0, low) + mid)
                w_high = 0.5 * (jnp.where(at_high[axis], 0.0, high) + mid)
                total = total + (jnp.maximum(w_high, 0.0) - jnp.minimum(w_low, 0.0))
                coef[i, t, 3 + 2 * axis] = jnp.where(
                    at_low[axis], 0.0, dt * jnp.maximum(w_low, 0.0)
                )
                coef[i, t, 4 + 2 * axis] = jnp.where(
                    at_high[axis], 0.0, -dt * jnp.minimum(w_high, 0.0)
                )
            coef[i, t, 0] = 1.0 - dt * total

    def transport(i, u_at, store):
        @pl.loop(0, QP // 2)
        def _(pair):
            for r in range(2):
                t = pair * 2 + r
                u = u_at(t + 1)
                x_low, x_high = shifted(u, 0)
                y_low, y_high = shifted(u, 1)
                near = coef[i, t, 0] * u + lam[0, i, t + 1]
                z_part = coef[i, t, 1] * u_at(t) + coef[i, t, 2] * u_at(t + 2)
                x_part = coef[i, t, 3] * x_low + coef[i, t, 4] * x_high
                y_part = coef[i, t, 5] * y_low + coef[i, t, 6] * y_high
                store(t, (near + z_part) + (x_part + y_part))

    for k in range(1, STEPS + 1):
        def result(i):
            def store(t, value):
                if k < STEPS:
                    lam[k, i, t + 1] = value
                else:
                    adj[i, t] = value

            return store

        edges_arrived(2 * k - 1, rest_edges(k - 1))
        for i in range(GROUP - 1):
            transport(i, lambda t: lam[k - 1, i + 1, t], result(i))
            if i == 0 and k < STEPS:
                send_first(k)
        if k == 3:
            gathered(3, lambda i: img.at[i, inner])
            send_edges(IMG_SLOT, img_edges, img_edges, base)
        first_arrived(k - 1)
        transport(GROUP - 1, lambda t: lam_in[k - 1, t], result(GROUP - 1))
        if k < STEPS:
            send_rest(k)

    for i in range(GROUP):
        send(
            adj.at[i],
            adj_out.at[0, pl.ds(QP * q, QP)],
            adj_send.at[i],
            adj_recv.at[q],
            (base + i, other),
        )
    edges_arrived(IMG_SLOT, img_edges)

    chunks = [(dim, half) for dim in range(3) for half in range(HALVES)]
    for number, (dim, half) in enumerate(chunks):
        @pl.loop(0, CP)
        def _(step):
            t = half * CP + step
            for i in range(GROUP):
                if dim == 0:
                    low = img[i, t] * jnp.where(t == 0, not_first, 1.0)
                    high = img[i, t + 2] * jnp.where(t == QP - 1, not_last, 1.0)
                    speed = v0[i, t + 1]
                else:
                    low, high = shifted(img[i, t + 1], dim - 1)
                    low = jnp.where(at_low[dim - 1], 0.0, low)
                    high = jnp.where(at_high[dim - 1], 0.0, high)
                    speed = v12[i, dim - 1, t]
                des[dim, i, t] = speed - adj[i, t] * (0.5 * (high - low))

        part = (dim, slice(None), pl.ds(half * CP, CP))
        for way, there in ((0, upper_base), (1, lower_base)):
            send(
                des.at[part],
                des_far.at[(way,) + part],
                d_send.at[way, number],
                d_recv.at[way, number],
                (there + q, slab),
            )

    for number, (dim, half) in enumerate(chunks):
        part = (dim, slice(None), pl.ds(half * CP, CP))
        for way in range(2):
            arrived(des_far.at[(way,) + part], d_send.at[way, number], d_recv.at[way, number])

        @pl.loop(0, CP)
        def _(step):
            t = half * CP + step
            line = [des_far[0, dim, i, t] for i in range(GROUP)]
            line += [des[dim, i, t] for i in range(GROUP)]
            line += [des_far[1, dim, i, t] for i in range(GROUP)]
            for i in range(GROUP):
                c = GROUP + i
                value = FRAME_WEIGHTS[0] * line[c]
                for k in range(1, TAPS + 1):
                    value = value + FRAME_WEIGHTS[k] * (line[c + k] + line[c - k])
                smo[dim, i, t] = value

        for i in range(GROUP):
            send(
                smo.at[dim, i, pl.ds(half * CP, CP)],
                smo_out.at[0, dim, pl.ds(QP * q + half * CP, CP)],
                o_send.at[number, i],
                o_recv.at[number, q],
                (base + i, other),
            )

    for j in range(GROUP):
        arrived(adj_out.at[0, pl.ds(QP * j, QP)], adj_send.at[j], adj_recv.at[j])
    for number, (dim, half) in enumerate(chunks):
        for j in range(GROUP):
            arrived(
                smo_out.at[0, dim, pl.ds(QP * j + half * CP, CP)],
                o_send.at[number, j],
                o_recv.at[number, j],
            )
    for copy in started:
        copy.wait_send()


def solution(mesh):
    phases, slabs = mesh.shape["phase"], mesh.shape["gz"]

    def local(velocity, image, target):
        f32 = jnp.float32
        vmem = lambda *lead: pltpu.VMEM(lead + (XW, YW), f32)
        dma = pltpu.SemaphoreType.DMA
        planes = image.shape[1]
        chunks = 3 * HALVES
        anywhere = pl.BlockSpec(memory_space=pl.ANY)
        return pl.pallas_call(
            functools.partial(kernel, phases, slabs),
            out_shape=(
                jax.ShapeDtypeStruct(image.shape, f32),
                jax.ShapeDtypeStruct(velocity.shape, f32),
            ),
            in_specs=[anywhere] * 3,
            out_specs=(anywhere, anywhere),
            scratch_shapes=[
                vmem(planes),
                vmem(planes),
                vmem(planes),
                vmem(GROUP, QP + 2),
                vmem(GROUP, 2, QP),
                vmem(GROUP, QP + 2),
                vmem(STEPS, GROUP, QP + 2),
                vmem(STEPS, QP + 2),
                vmem(GROUP, QP, 7),
                vmem(GROUP, QP),
                vmem(3, GROUP, QP),
                vmem(2, 3, GROUP, QP),
                vmem(3, GROUP, QP),
                dma((2,)),
                dma((4, GROUP)),
                dma((4, GROUP)),
                dma((2 * STEPS + 2, 2)),
                dma((2 * STEPS + 2, 2)),
                dma((STEPS,)),
                dma((STEPS,)),
                dma((GROUP,)),
                dma((GROUP,)),
                dma((2, chunks)),
                dma((2, chunks)),
                dma((chunks, GROUP)),
                dma((chunks, GROUP)),
            ],
            compiler_params=pltpu.CompilerParams(
                collective_id=0,
                has_side_effects=True,
                vmem_limit_bytes=40 * 1024 * 1024,
            ),
        )(velocity, image, target)

    return jax.shard_map(
        local,
        mesh=mesh,
        in_specs=(
            P("phase", None, "gz", None, None),
            P("phase", "gz", None, None),
            P("phase", "gz", None, None),
        ),
        out_specs=(P("phase", "gz", None, None), P("phase", None, "gz", None, None)),
        check_vma=False,
    )
```

time: 247 us -> 110 us (0.45)
  waiting for transfers between devices: 129 us -> 0 us
  Pallas kernels: 0 us -> 103 us
  starting transfers between devices: 98.3 us -> 0 us
  other arithmetic: 16.9 us -> 0 us
  local copies, waits for them, and re-layouts: 0.45 us -> 5.42 us
    ppermute x22 -> x0, waiting for transfers between devices: 129 us -> none  [the longest x12 115 us: passed_along(): return lax.ppermute(block, axis, route)]
    pallas_call x0 -> x1, Pallas kernels: none -> 103 us  [local(): pl.pallas_call(functools.partial(kernel, phases, slabs), out_shape=(jax.S...]
    ppermute x22 -> x0, starting transfers between devices: 98.3 us -> none  [the longest x12 72.3 us: passed_along(): return lax.ppermute(block, axis, route)]
    add x16 -> x0, other arithmetic: 6.38 us -> none  [the longest x12 5.13 us: transport(): jnp.maximum(face_speed, 0.0) * lower_cell]
    concatenate x5 -> x0, other arithmetic: 6.36 us -> none  [padded(): block = jnp.concatenate([low, block, high], axis=dim)]
    unnamed x8, local copies, waits for them, and re-layouts: 0.02 us -> 5.42 us
  transfers between devices with their start and end apart: 22 -> 0, of which waited for: 15 -> 0; matrix products, arithmetic and copies ran while one was open for 2% -> 0% of each run, Pallas kernels for 0% -> 0%
where the time goes in v1:
time: 110 us
  Pallas kernels  103 us (94%)
  local copies, waits for them, and re-layouts  5.42 us (5%)
    pallas_call x1, Pallas kernels, local(): pl.pallas_call(functools.partial(kernel, phases, slabs), out_shape=(jax.S...  103 us
    unnamed x8, local copies, waits for them, and re-layouts  5.42 us

profile of v1, /device:TPU:1, one launch (start us, length us, event | category | flops | bytes accessed | tf_op | source)
XLA Modules:
  0.0 109.6 jit_solution(1269238368379797431)
XLA Ops:
  0.6 0.0 copy-start
  0.6 1.4 %copy-done = f32[1,3,64,16,128]{4,3,2,1,0:T(8,128)S(1)} copy-done((f32[1,3,64,16,128]{4,3,2,1,0:T(8,128)S(1)}, f32[1,3,64,16,128]{4,3,2,1,0:T(8,128)}, u32[]{:S(2)}) %copy-start) | copy-done | bytes 1572888
  2.0 0.0 copy-start.1
  2.0 1.0 copy-done.1
  3.1 0.0 copy-start.2
  3.1 1.0 copy-done.2
  4.1 103.5 %shard_map.50 = (f32[1,64,16,128]{3,2,1,0:T(8,128)S(1)}, f32[1,3,64,16,128]{4,3,2,1,0:T(8,128)S(1)}) custom-call(f32[1,3,64,16,128]{4,3,2,1,0:T(8,128)S(1)} %copy-done, f32[1,64,16,128]{3,2,1,0:T(8,128)S(1)} %copy-done.1, f32[1,64,16,128]{3,2,1,0:T(8,128)S(1)} %copy-done.2), custom_call_target="tpu_custom_call" | custom-call | tf_op jit(solution)/shard_map/pallas_call | solution.py:367
  107.6 0.8 copy.7
  108.4 1.1 %copy.8 = f32[1,3,64,16,128]{4,3,2,1,0:T(8,128)} copy(f32[1,3,64,16,128]{4,3,2,1,0:T(8,128)S(1)} %get-tuple-element.5) | data formatting | bytes 3145728
Async XLA Ops:
  0.6 1.4 %copy-start = (f32[1,3,64,16,128]{4,3,2,1,0:T(8,128)S(1)}, f32[1,3,64,16,128]{4,3,2,1,0:T(8,128)}, u32[]{:S(2)}) copy-start(f32[1,3,64,16,128]{4,3,2,1,0:T(8,128)} %v_ref.1) | copy-start | bytes 4718596
  2.0 1.0 copy-start.1
  3.1 1.0 copy-start.2

commit v2 on v1

--- a/solution.py
+++ b/solution.py
@@ -167,7 +167,7 @@
         arrived(dest(QP + 1), edge_send.at[slot, 0], edge_recv.at[slot, 0])
         arrived(dest(0), edge_send.at[slot, 1], edge_recv.at[slot, 1])
 
-    def send_first(k):
+    def send_main(k):
         send(
             lam.at[k, 0, inner],
             lam_in.at[k, inner],
@@ -175,32 +175,33 @@
             lz_recv.at[k],
             (lower_base + q, slab),
         )
+
+    def lam_edges(k, i):
+        if i == 0:
+            return lambda plane: lam_in.at[k, plane]
+        return lambda plane: lam.at[k, i, plane]
+
+    def send_lam_edges(k, i):
         send_edges(
-            2 * k,
-            lambda plane: lam.at[k, 0, plane],
-            lambda plane: lam_in.at[k, plane],
-            lower_base,
-        )
-
-    def first_arrived(k):
-        arrived(lam_in.at[k, inner], lz_send.at[k], lz_recv.at[k])
-        edges_arrived(2 * k, lambda plane: lam_in.at[k, plane])
-
-    def rest_edges(k):
-        return lambda plane: lam.at[k, pl.ds(1, GROUP - 1), plane]
-
-    def send_rest(k):
-        send_edges(2 * k + 1, rest_edges(k), rest_edges(k), base)
+            GROUP * k + i,
+            lambda plane: lam.at[k, i, plane],
+            lam_edges(k, i),
+            lower_base if i == 0 else base,
+        )
+
+    def lam_edges_arrived(k, i):
+        edges_arrived(GROUP * k + i, lam_edges(k, i))
 
     v0_edges = lambda plane: v0.at[:, plane]
     img_edges = lambda plane: img.at[:, plane]
-    V_SLOT, IMG_SLOT = 2 * STEPS, 2 * STEPS + 1
+    V_SLOT, IMG_SLOT = GROUP * STEPS, GROUP * STEPS + 1
 
     gathered(0, lambda i: v0.at[i, inner])
     send_edges(V_SLOT, v0_edges, v0_edges, base)
     gathered(1, lambda i: lam.at[0, i, inner])
-    send_first(0)
-    send_rest(0)
+    send_main(0)
+    for i in range(GROUP):
+        send_lam_edges(0, i)
     edges_arrived(V_SLOT, v0_edges)
     gathered(2, lambda i: v12.at[i])
 
@@ -240,42 +241,51 @@
                 )
             coef[i, t, 0] = 1.0 - dt * total
 
-    def transport(i, u_at, store):
-        @pl.loop(0, QP // 2)
-        def _(pair):
-            for r in range(2):
-                t = pair * 2 + r
-                u = u_at(t + 1)
-                x_low, x_high = shifted(u, 0)
-                y_low, y_high = shifted(u, 1)
-                near = coef[i, t, 0] * u + lam[0, i, t + 1]
-                z_part = coef[i, t, 1] * u_at(t) + coef[i, t, 2] * u_at(t + 2)
-                x_part = coef[i, t, 3] * x_low + coef[i, t, 4] * x_high
-                y_part = coef[i, t, 5] * y_low + coef[i, t, 6] * y_high
-                store(t, (near + z_part) + (x_part + y_part))
-
-    for k in range(1, STEPS + 1):
-        def result(i):
-            def store(t, value):
-                if k < STEPS:
-                    lam[k, i, t + 1] = value
-                else:
-                    adj[i, t] = value
-
-            return store
-
-        edges_arrived(2 * k - 1, rest_edges(k - 1))
-        for i in range(GROUP - 1):
-            transport(i, lambda t: lam[k - 1, i + 1, t], result(i))
-            if i == 0 and k < STEPS:
-                send_first(k)
-        if k == 3:
+    def transport(i, t, u_at, store):
+        u = u_at(t + 1)
+        x_low, x_high = shifted(u, 0)
+        y_low, y_high = shifted(u, 1)
+        near = coef[i, t, 0] * u + lam[0, i, t + 1]
+        z_part = coef[i, t, 1] * u_at(t) + coef[i, t, 2] * u_at(t + 2)
+        x_part = coef[i, t, 3] * x_low + coef[i, t, 4] * x_high
+        y_part = coef[i, t, 5] * y_low + coef[i, t, 6] * y_high
+        store(t, (near + z_part) + (x_part + y_part))
+
+    def advance(k, i):
+        def u_at(plane):
+            return lam_in[k - 1, plane] if i == GROUP - 1 else lam[k - 1, i + 1, plane]
+
+        def store(t, value):
+            if k < STEPS:
+                lam[k, i, t + 1] = value
+            else:
+                adj[i, t] = value
+
+        if i == GROUP - 1:
+            arrived(lam_in.at[k - 1, inner], lz_send.at[k - 1], lz_recv.at[k - 1])
+        lam_edges_arrived(k - 1, (i + 1) % GROUP)
+        for t in (0, QP - 1):
+            transport(i, t, u_at, store)
+        if k < STEPS:
+            send_lam_edges(k, i)
+
+        @pl.loop(0, 2)
+        def _(part):
+            for r in range(QP // 2 - 1):
+                transport(i, 1 + part * (QP // 2 - 1) + r, u_at, store)
+
+        if k < STEPS and i == 0:
+            send_main(k)
+
+    order = (
+        [(1, 0), (1, 1), (1, 2), (1, 3), (2, 0), (2, 1), (2, 2), (3, 0), (3, 1), (2, 3)]
+        + [(4, 0), (3, 2), (3, 3), (4, 1), (4, 2), (4, 3)]
+    )
+    for k, i in order:
+        if (k, i) == (2, 3):
             gathered(3, lambda i: img.at[i, inner])
             send_edges(IMG_SLOT, img_edges, img_edges, base)
-        first_arrived(k - 1)
-        transport(GROUP - 1, lambda t: lam_in[k - 1, t], result(GROUP - 1))
-        if k < STEPS:
-            send_rest(k)
+        advance(k, i)
 
     for i in range(GROUP):
         send(
@@ -289,10 +299,9 @@
 
     chunks = [(dim, half) for dim in range(3) for half in range(HALVES)]
     for number, (dim, half) in enumerate(chunks):
-        @pl.loop(0, CP)
+        @pl.loop(0, CP // 4)
         def _(step):
-            t = half * CP + step
-            for i in range(GROUP):
+            for t, i in [(half * CP + step * 4 + r, i) for r in range(4) for i in range(GROUP)]:
                 if dim == 0:
                     low = img[i, t] * jnp.where(t == 0, not_first, 1.0)
                     high = img[i, t + 2] * jnp.where(t == QP - 1, not_last, 1.0)
@@ -319,18 +328,19 @@
         for way in range(2):
             arrived(des_far.at[(way,) + part], d_send.at[way, number], d_recv.at[way, number])
 
-        @pl.loop(0, CP)
+        @pl.loop(0, CP // 2)
         def _(step):
-            t = half * CP + step
-            line = [des_far[0, dim, i, t] for i in range(GROUP)]
-            line += [des[dim, i, t] for i in range(GROUP)]
-            line += [des_far[1, dim, i, t] for i in range(GROUP)]
-            for i in range(GROUP):
-                c = GROUP + i
-                value = FRAME_WEIGHTS[0] * line[c]
-                for k in range(1, TAPS + 1):
-                    value = value + FRAME_WEIGHTS[k] * (line[c + k] + line[c - k])
-                smo[dim, i, t] = value
+            for r in range(2):
+                t = half * CP + step * 2 + r
+                line = [des_far[0, dim, i, t] for i in range(GROUP)]
+                line += [des[dim, i, t] for i in range(GROUP)]
+                line += [des_far[1, dim, i, t] for i in range(GROUP)]
+                for i in range(GROUP):
+                    c = GROUP + i
+                    value = FRAME_WEIGHTS[0] * line[c]
+                    for k in range(1, TAPS + 1):
+                        value = value + FRAME_WEIGHTS[k] * (line[c + k] + line[c - k])
+                    smo[dim, i, t] = value
 
         for i in range(GROUP):
             send(
@@ -389,8 +399,8 @@
                 dma((2,)),
                 dma((4, GROUP)),
                 dma((4, GROUP)),
-                dma((2 * STEPS + 2, 2)),
-                dma((2 * STEPS + 2, 2)),
+                dma((GROUP * STEPS + 2, 2)),
+                dma((GROUP * STEPS + 2, 2)),
                 dma((STEPS,)),
                 dma((STEPS,)),
                 dma((GROUP,)),
@@ -405,7 +415,7 @@
                 has_side_effects=True,
                 vmem_limit_bytes=40 * 1024 * 1024,
             ),
-        )(velocity, image, target)
+        )(*(pltpu.with_memory_space_constraint(a, pltpu.HBM) for a in (velocity, image, target)))
 
     return jax.shard_map(
         local,

time: 110 us -> 102 us (0.927)
  Pallas kernels: 103 us -> 99.4 us
  local copies, waits for them, and re-layouts: 5.42 us -> 1.94 us
    pallas_call x1, Pallas kernels: 103 us -> 99.4 us  [local(): pl.pallas_call(functools.partial(kernel, phases, slabs), out_shape=(jax.S...]
    unnamed x8 -> x2, local copies, waits for them, and re-layouts: 5.42 us -> 1.94 us
where the time goes in v2:
time: 102 us
  Pallas kernels  99.4 us (97%)
  local copies, waits for them, and re-layouts  1.94 us (2%)
    pallas_call x1, Pallas kernels, local(): pl.pallas_call(functools.partial(kernel, phases, slabs), out_shape=(jax.S...  99.4 us

profile of v2, /device:TPU:1, one launch (start us, length us, event | category | flops | bytes accessed | tf_op | source)
XLA Modules:
  0.0 101.9 jit_solution(8226027083627651140)
XLA Ops:
  0.6 99.4 %shard_map.50 = (f32[1,64,16,128]{3,2,1,0:T(8,128)S(1)}, f32[1,3,64,16,128]{4,3,2,1,0:T(8,128)S(1)}) custom-call(f32[1,3,64,16,128]{4,3,2,1,0:T(8,128)} %v_ref.1, f32[1,64,16,128]{3,2,1,0:T(8,128)} %img_ref.1, f32[1,64,16,128]{3,2,1,0:T(8,128)} %tgt_ref.1), custom_call_target="tpu_custom_call" | custom-call | tf_op jit(solution)/shard_map/pallas_call | solution.py:377
  100.0 0.8 copy.7
  100.8 1.1 %copy.8 = f32[1,3,64,16,128]{4,3,2,1,0:T(8,128)} copy(f32[1,3,64,16,128]{4,3,2,1,0:T(8,128)S(1)} %get-tuple-element.5) | data formatting | bytes 3145728

commit v3 on v2

--- a/solution.py
+++ b/solution.py
@@ -20,8 +20,9 @@
 GROUP = 4
 QP = 16
 XW, YW = 16, 128
-HALVES = 2
-CP = QP // HALVES
+EARLY = QP // 2
+CP = 4
+PIECE = 2
 
 
 def flip(g):
@@ -39,8 +40,7 @@
     img_own,
     tgt_own,
     s_own,
-    v0,
-    v12,
+    vel,
     img,
     lam,
     lam_in,
@@ -48,6 +48,9 @@
     adj,
     des,
     des_far,
+    vel_far,
+    img_far,
+    adj_far,
     smo,
     load_sem,
     in_send,
@@ -134,7 +137,13 @@
             arrived(dest(i), in_send.at[field, i], in_recv.at[field, i])
 
     inner = pl.ds(1, QP)
-    scatter(0, lambda j: v_ref.at[0, 0, pl.ds(QP * j, QP)], v0.at[q, inner])
+    scatter(0, lambda j: v_ref.at[0, 0, pl.ds(QP * j, QP)], vel.at[q, 0, inner])
+    for axis in (1, 2):
+        scatter(
+            axis,
+            lambda j: v_ref.at[0, axis, pl.ds(QP * j, EARLY)],
+            vel.at[q, axis, pl.ds(1, EARLY)],
+        )
     for load in loads:
         load.wait()
 
@@ -143,9 +152,34 @@
         for r in range(GROUP):
             s_own[t * GROUP + r] = img_own[t * GROUP + r] - tgt_own[t * GROUP + r]
 
-    scatter(1, lambda j: s_own.at[pl.ds(QP * j, QP)], lam.at[0, q, inner])
-    scatter(2, lambda j: v_ref.at[0, pl.ds(1, 2), pl.ds(QP * j, QP)], v12.at[q])
-    scatter(3, lambda j: img_ref.at[0, pl.ds(QP * j, QP)], img.at[q, inner])
+    scatter(3, lambda j: s_own.at[pl.ds(QP * j, QP)], lam.at[0, q, inner])
+    late = pl.ds(1 + EARLY, QP - EARLY)
+    scatter(
+        4,
+        lambda j: v_ref.at[0, pl.ds(1, 2), pl.ds(QP * j + EARLY, QP - EARLY)],
+        vel.at[q, pl.ds(1, 2), late],
+    )
+
+    def scatter_image(piece):
+        scatter(
+            5 + piece,
+            lambda j: img_ref.at[0, pl.ds(QP * j + PIECE * piece, PIECE)],
+            img.at[q, pl.ds(1 + PIECE * piece, PIECE)],
+        )
+
+    def forward(number, source, dest, ways=(0, 1)):
+        for way in ways:
+            send(
+                source,
+                dest(way),
+                d_send.at[way, number],
+                d_recv.at[way, number],
+                ((upper_base, lower_base)[way] + q, slab),
+            )
+
+    def forwarded(number, dest):
+        for way in range(2):
+            arrived(dest(way), d_send.at[way, number], d_recv.at[way, number])
 
     def send_edges(slot, buffer, dest, here):
         send(
@@ -192,18 +226,29 @@
     def lam_edges_arrived(k, i):
         edges_arrived(GROUP * k + i, lam_edges(k, i))
 
-    v0_edges = lambda plane: v0.at[:, plane]
+    v0_edges = lambda plane: vel.at[:, 0, plane]
     img_edges = lambda plane: img.at[:, plane]
     V_SLOT, IMG_SLOT = GROUP * STEPS, GROUP * STEPS + 1
 
-    gathered(0, lambda i: v0.at[i, inner])
+    def forward_velocity(axis, ways):
+        forward(
+            axis, vel.at[:, axis, pl.ds(1, EARLY)], lambda way: vel_far.at[way, :, axis], ways
+        )
+
+    gathered(0, lambda i: vel.at[i, 0, inner])
+    forward_velocity(0, (0, 1))
     send_edges(V_SLOT, v0_edges, v0_edges, base)
-    gathered(1, lambda i: lam.at[0, i, inner])
+    gathered(1, lambda i: vel.at[i, 1, pl.ds(1, EARLY)])
+    forward_velocity(1, (0, 1))
+    gathered(2, lambda i: vel.at[i, 2, pl.ds(1, EARLY)])
+    forward_velocity(2, (0,))
+    gathered(3, lambda i: lam.at[0, i, inner])
     send_main(0)
     for i in range(GROUP):
         send_lam_edges(0, i)
+    forward_velocity(2, (1,))
     edges_arrived(V_SLOT, v0_edges)
-    gathered(2, lambda i: v12.at[i])
+    gathered(4, lambda i: vel.at[i, pl.ds(1, 2), late])
 
     row = lax.broadcasted_iota(jnp.int32, (XW, YW), 0)
     lane = lax.broadcasted_iota(jnp.int32, (XW, YW), 1)
@@ -221,14 +266,14 @@
         keep_low = jnp.where(t == 0, not_first, 1.0)
         keep_high = jnp.where(t == QP - 1, not_last, 1.0)
         for i in range(GROUP):
-            mid = v0[i, t + 1]
-            w_low = 0.5 * (v0[i, t] * keep_low + mid)
-            w_high = 0.5 * (v0[i, t + 2] * keep_high + mid)
+            mid = vel[i, 0, t + 1]
+            w_low = 0.5 * (vel[i, 0, t] * keep_low + mid)
+            w_high = 0.5 * (vel[i, 0, t + 2] * keep_high + mid)
             total = jnp.maximum(w_high, 0.0) - jnp.minimum(w_low, 0.0)
             coef[i, t, 1] = (dt * keep_low) * jnp.maximum(w_low, 0.0)
             coef[i, t, 2] = (-dt * keep_high) * jnp.minimum(w_high, 0.0)
             for axis in range(2):
-                mid = v12[i, axis, t]
+                mid = vel[i, axis + 1, t + 1]
                 low, high = shifted(mid, axis)
                 w_low = 0.5 * (jnp.where(at_low[axis], 0.0, low) + mid)
                 w_high = 0.5 * (jnp.where(at_high[axis], 0.0, high) + mid)
@@ -281,12 +326,21 @@
         [(1, 0), (1, 1), (1, 2), (1, 3), (2, 0), (2, 1), (2, 2), (3, 0), (3, 1), (2, 3)]
         + [(4, 0), (3, 2), (3, 3), (4, 1), (4, 2), (4, 3)]
     )
-    for k, i in order:
-        if (k, i) == (2, 3):
-            gathered(3, lambda i: img.at[i, inner])
+    pieces = QP // PIECE
+    near_image = pl.ds(0, EARLY + 2)
+    for turn, (k, i) in enumerate(order):
+        advance(k, i)
+        if turn < pieces:
+            scatter_image(turn)
+        if (k, i) == (3, 2):
+            for piece in range(pieces):
+                gathered(5 + piece, lambda i: img.at[i, pl.ds(1 + PIECE * piece, PIECE)])
             send_edges(IMG_SLOT, img_edges, img_edges, base)
-        advance(k, i)
-
+        if (k, i) == (4, 1):
+            edges_arrived(IMG_SLOT, img_edges)
+            forward(3, img.at[:, near_image], lambda way: img_far.at[way])
+
+    forward(4, adj.at[:, pl.ds(0, EARLY)], lambda way: adj_far.at[way])
     for i in range(GROUP):
         send(
             adj.at[i],
@@ -295,43 +349,32 @@
             adj_recv.at[q],
             (base + i, other),
         )
-    edges_arrived(IMG_SLOT, img_edges)
-
-    chunks = [(dim, half) for dim in range(3) for half in range(HALVES)]
-    for number, (dim, half) in enumerate(chunks):
-        @pl.loop(0, CP // 4)
+
+    def descent(image_at, speed, state, dim, t):
+        if dim == 0:
+            low = image_at(t) * jnp.where(t == 0, not_first, 1.0)
+            high = image_at(t + 2) * jnp.where(t == QP - 1, not_last, 1.0)
+        else:
+            low, high = shifted(image_at(t + 1), dim - 1)
+            low = jnp.where(at_low[dim - 1], 0.0, low)
+            high = jnp.where(at_high[dim - 1], 0.0, high)
+        return speed - state * (0.5 * (high - low))
+
+    def own_descent(dim, start, count):
+        @pl.loop(0, count // 4)
         def _(step):
-            for t, i in [(half * CP + step * 4 + r, i) for r in range(4) for i in range(GROUP)]:
-                if dim == 0:
-                    low = img[i, t] * jnp.where(t == 0, not_first, 1.0)
-                    high = img[i, t + 2] * jnp.where(t == QP - 1, not_last, 1.0)
-                    speed = v0[i, t + 1]
-                else:
-                    low, high = shifted(img[i, t + 1], dim - 1)
-                    low = jnp.where(at_low[dim - 1], 0.0, low)
-                    high = jnp.where(at_high[dim - 1], 0.0, high)
-                    speed = v12[i, dim - 1, t]
-                des[dim, i, t] = speed - adj[i, t] * (0.5 * (high - low))
-
-        part = (dim, slice(None), pl.ds(half * CP, CP))
-        for way, there in ((0, upper_base), (1, lower_base)):
-            send(
-                des.at[part],
-                des_far.at[(way,) + part],
-                d_send.at[way, number],
-                d_recv.at[way, number],
-                (there + q, slab),
-            )
-
-    for number, (dim, half) in enumerate(chunks):
-        part = (dim, slice(None), pl.ds(half * CP, CP))
-        for way in range(2):
-            arrived(des_far.at[(way,) + part], d_send.at[way, number], d_recv.at[way, number])
-
-        @pl.loop(0, CP // 2)
+            for r in range(4):
+                t = start + step * 4 + r
+                for i in range(GROUP):
+                    des[dim, i, t] = descent(
+                        lambda plane: img[i, plane], vel[i, dim, t + 1], adj[i, t], dim, t
+                    )
+
+    def smooth(number, dim, start, count):
+        @pl.loop(0, count // 2)
         def _(step):
             for r in range(2):
-                t = half * CP + step * 2 + r
+                t = start + step * 2 + r
                 line = [des_far[0, dim, i, t] for i in range(GROUP)]
                 line += [des[dim, i, t] for i in range(GROUP)]
                 line += [des_far[1, dim, i, t] for i in range(GROUP)]
@@ -344,19 +387,54 @@
 
         for i in range(GROUP):
             send(
-                smo.at[dim, i, pl.ds(half * CP, CP)],
-                smo_out.at[0, dim, pl.ds(QP * q + half * CP, CP)],
+                smo.at[dim, i, pl.ds(start, count)],
+                smo_out.at[0, dim, pl.ds(QP * q + start, count)],
                 o_send.at[number, i],
                 o_recv.at[number, q],
                 (base + i, other),
             )
 
+    early_chunks = [(dim, 0, EARLY) for dim in range(3)]
+    late_chunks = [(dim, start, CP) for dim in range(3) for start in range(EARLY, QP, CP)]
+    chunks = early_chunks + late_chunks
+    for number, (dim, start, count) in enumerate(late_chunks):
+        own_descent(dim, start, count)
+        part = (dim, slice(None), pl.ds(start, count))
+        forward(5 + number, des.at[part], lambda way: des_far.at[(way,) + part])
+    for dim in range(3):
+        own_descent(dim, 0, EARLY)
+
+    for axis in range(3):
+        forwarded(axis, lambda way: vel_far.at[way, :, axis])
+    forwarded(3, lambda way: img_far.at[way])
+    forwarded(4, lambda way: adj_far.at[way])
+    for number, (dim, start, count) in enumerate(early_chunks):
+        for way in range(2):
+            @pl.loop(0, EARLY // 4)
+            def _(step):
+                for r in range(4):
+                    t = step * 4 + r
+                    for i in range(GROUP):
+                        des_far[way, dim, i, t] = descent(
+                            lambda plane: img_far[way, i, plane],
+                            vel_far[way, i, dim, t],
+                            adj_far[way, i, t],
+                            dim,
+                            t,
+                        )
+
+        smooth(number, dim, start, count)
+    for number, (dim, start, count) in enumerate(late_chunks):
+        part = (dim, slice(None), pl.ds(start, count))
+        forwarded(5 + number, lambda way: des_far.at[(way,) + part])
+        smooth(len(early_chunks) + number, dim, start, count)
+
     for j in range(GROUP):
         arrived(adj_out.at[0, pl.ds(QP * j, QP)], adj_send.at[j], adj_recv.at[j])
-    for number, (dim, half) in enumerate(chunks):
+    for number, (dim, start, count) in enumerate(chunks):
         for j in range(GROUP):
             arrived(
-                smo_out.at[0, dim, pl.ds(QP * j + half * CP, CP)],
+                smo_out.at[0, dim, pl.ds(QP * j + start, count)],
                 o_send.at[number, j],
                 o_recv.at[number, j],
             )
@@ -372,7 +450,9 @@
         vmem = lambda *lead: pltpu.VMEM(lead + (XW, YW), f32)
         dma = pltpu.SemaphoreType.DMA
         planes = image.shape[1]
-        chunks = 3 * HALVES
+        late_chunks = 3 * (QP - EARLY) // CP
+        chunks = 3 + late_chunks
+        fields = 5 + QP // PIECE
         anywhere = pl.BlockSpec(memory_space=pl.ANY)
         return pl.pallas_call(
             functools.partial(kernel, phases, slabs),
@@ -386,8 +466,7 @@
                 vmem(planes),
                 vmem(planes),
                 vmem(planes),
-                vmem(GROUP, QP + 2),
-                vmem(GROUP, 2, QP),
+                vmem(GROUP, 3, QP + 2),
                 vmem(GROUP, QP + 2),
                 vmem(STEPS, GROUP, QP + 2),
                 vmem(STEPS, QP + 2),
@@ -395,18 +474,21 @@
                 vmem(GROUP, QP),
                 vmem(3, GROUP, QP),
                 vmem(2, 3, GROUP, QP),
+                vmem(2, GROUP, 3, EARLY),
+                vmem(2, GROUP, EARLY + 2),
+                vmem(2, GROUP, EARLY),
                 vmem(3, GROUP, QP),
                 dma((2,)),
-                dma((4, GROUP)),
-                dma((4, GROUP)),
+                dma((fields, GROUP)),
+                dma((fields, GROUP)),
                 dma((GROUP * STEPS + 2, 2)),
                 dma((GROUP * STEPS + 2, 2)),
                 dma((STEPS,)),
                 dma((STEPS,)),
                 dma((GROUP,)),
                 dma((GROUP,)),
-                dma((2, chunks)),
-                dma((2, chunks)),
+                dma((2, 5 + late_chunks)),
+                dma((2, 5 + late_chunks)),
                 dma((chunks, GROUP)),
                 dma((chunks, GROUP)),
             ],

time: 102 us -> 93.5 us (0.917)
  Pallas kernels: 99.4 us -> 90.9 us
    pallas_call x1, Pallas kernels: 99.4 us -> 90.9 us  [local(): pl.pallas_call(functools.partial(kernel, phases, slabs), out_shape=(jax.S...]
where the time goes in v3:
time: 93.5 us; the launch traced here: 93.4 us
  Pallas kernels  90.9 us (97%)
  local copies, waits for them, and re-layouts  1.94 us (2%)
    pallas_call x1, Pallas kernels, local(): pl.pallas_call(functools.partial(kernel, phases, slabs), out_shape=(jax.S...  90.9 us
    unnamed x2, local copies, waits for them, and re-layouts  1.94 us

profile of v3, /device:TPU:1, one launch (start us, length us, event | category | flops | bytes accessed | tf_op | source)
XLA Modules:
  0.0 93.4 jit_solution(1703776802583025069)
XLA Ops:
  0.6 90.9 %shard_map.50 = (f32[1,64,16,128]{3,2,1,0:T(8,128)S(1)}, f32[1,3,64,16,128]{4,3,2,1,0:T(8,128)S(1)}) custom-call(f32[1,3,64,16,128]{4,3,2,1,0:T(8,128)} %v_ref.1, f32[1,64,16,128]{3,2,1,0:T(8,128)} %img_ref.1, f32[1,64,16,128]{3,2,1,0:T(8,128)} %tgt_ref.1), custom_call_target="tpu_custom_call" | custom-call | tf_op jit(solution)/shard_map/pallas_call | solution.py:457
  91.5 0.8 copy.7
  92.3 1.1 %copy.8 = f32[1,3,64,16,128]{4,3,2,1,0:T(8,128)} copy(f32[1,3,64,16,128]{4,3,2,1,0:T(8,128)S(1)} %get-tuple-element.5) | data formatting | bytes 3145728

commit v4 on v3

--- a/solution.py
+++ b/solution.py
@@ -21,7 +21,8 @@
 QP = 16
 XW, YW = 16, 128
 EARLY = QP // 2
-CP = 4
+LATE_CHUNKS = [(dim, start, 4) for dim in range(3) for start in range(EARLY, QP, 4)]
+LATE_CHUNKS[-1:] = [(2, QP - 4, 2), (2, QP - 2, 2)]
 PIECE = 2
 
 
@@ -137,13 +138,12 @@
             arrived(dest(i), in_send.at[field, i], in_recv.at[field, i])
 
     inner = pl.ds(1, QP)
-    scatter(0, lambda j: v_ref.at[0, 0, pl.ds(QP * j, QP)], vel.at[q, 0, inner])
-    for axis in (1, 2):
-        scatter(
-            axis,
-            lambda j: v_ref.at[0, axis, pl.ds(QP * j, EARLY)],
-            vel.at[q, axis, pl.ds(1, EARLY)],
-        )
+    early, late = pl.ds(1, EARLY), pl.ds(1 + EARLY, QP - EARLY)
+    for axis in range(3):
+        scatter(axis, lambda j: v_ref.at[0, axis, pl.ds(QP * j, EARLY)], vel.at[q, axis, early])
+    scatter(
+        5, lambda j: v_ref.at[0, 0, pl.ds(QP * j + EARLY, QP - EARLY)], vel.at[q, 0, late]
+    )
     for load in loads:
         load.wait()
 
@@ -153,7 +153,6 @@
             s_own[t * GROUP + r] = img_own[t * GROUP + r] - tgt_own[t * GROUP + r]
 
     scatter(3, lambda j: s_own.at[pl.ds(QP * j, QP)], lam.at[0, q, inner])
-    late = pl.ds(1 + EARLY, QP - EARLY)
     scatter(
         4,
         lambda j: v_ref.at[0, pl.ds(1, 2), pl.ds(QP * j + EARLY, QP - EARLY)],
@@ -162,7 +161,7 @@
 
     def scatter_image(piece):
         scatter(
-            5 + piece,
+            6 + piece,
             lambda j: img_ref.at[0, pl.ds(QP * j + PIECE * piece, PIECE)],
             img.at[q, pl.ds(1 + PIECE * piece, PIECE)],
         )
@@ -231,22 +230,20 @@
     V_SLOT, IMG_SLOT = GROUP * STEPS, GROUP * STEPS + 1
 
     def forward_velocity(axis, ways):
-        forward(
-            axis, vel.at[:, axis, pl.ds(1, EARLY)], lambda way: vel_far.at[way, :, axis], ways
-        )
-
-    gathered(0, lambda i: vel.at[i, 0, inner])
-    forward_velocity(0, (0, 1))
+        forward(axis, vel.at[:, axis, early], lambda way: vel_far.at[way, :, axis], ways)
+
+    for axis in range(3):
+        gathered(axis, lambda i: vel.at[i, axis, early])
+        forward_velocity(axis, (0,) if axis == 2 else (0, 1))
+    gathered(5, lambda i: vel.at[i, 0, late])
     send_edges(V_SLOT, v0_edges, v0_edges, base)
-    gathered(1, lambda i: vel.at[i, 1, pl.ds(1, EARLY)])
-    forward_velocity(1, (0, 1))
-    gathered(2, lambda i: vel.at[i, 2, pl.ds(1, EARLY)])
-    forward_velocity(2, (0,))
     gathered(3, lambda i: lam.at[0, i, inner])
     send_main(0)
     for i in range(GROUP):
         send_lam_edges(0, i)
     forward_velocity(2, (1,))
+    scatter_image(0)
+    scatter_image(1)
     edges_arrived(V_SLOT, v0_edges)
     gathered(4, lambda i: vel.at[i, pl.ds(1, 2), late])
 
@@ -327,20 +324,32 @@
         + [(4, 0), (3, 2), (3, 3), (4, 1), (4, 2), (4, 3)]
     )
     pieces = QP // PIECE
-    near_image = pl.ds(0, EARLY + 2)
+    blocks = [(0, 2), (2, EARLY // PIECE + 1)]
+    block_planes = [pl.ds(1, 2 * PIECE), pl.ds(1 + 2 * PIECE, EARLY - 2 * PIECE + 1)]
+
+    def image_gathered(start, stop):
+        for piece in range(start, stop):
+            gathered(6 + piece, lambda i: img.at[i, pl.ds(1 + PIECE * piece, PIECE)])
+
+    def image_far(planes):
+        return lambda way: img_far.at[way, :, planes]
+
     for turn, (k, i) in enumerate(order):
         advance(k, i)
-        if turn < pieces:
-            scatter_image(turn)
-        if (k, i) == (3, 2):
-            for piece in range(pieces):
-                gathered(5 + piece, lambda i: img.at[i, pl.ds(1 + PIECE * piece, PIECE)])
+        if turn + 2 < pieces:
+            scatter_image(turn + 2)
+        if (k, i) in ((2, 0), (3, 0)):
+            block = k - 2
+            image_gathered(*blocks[block])
+            forward(3 + block, img.at[:, block_planes[block]], image_far(block_planes[block]))
+        if (k, i) == (2, 3):
+            image_gathered(blocks[1][1], pieces)
             send_edges(IMG_SLOT, img_edges, img_edges, base)
-        if (k, i) == (4, 1):
+        if (k, i) == (3, 3):
             edges_arrived(IMG_SLOT, img_edges)
-            forward(3, img.at[:, near_image], lambda way: img_far.at[way])
-
-    forward(4, adj.at[:, pl.ds(0, EARLY)], lambda way: adj_far.at[way])
+            forward(5, img.at[:, 0], image_far(0))
+
+    forward(6, adj.at[:, pl.ds(0, EARLY)], lambda way: adj_far.at[way])
     for i in range(GROUP):
         send(
             adj.at[i],
@@ -361,10 +370,12 @@
         return speed - state * (0.5 * (high - low))
 
     def own_descent(dim, start, count):
-        @pl.loop(0, count // 4)
+        size = min(count, 4)
+
+        @pl.loop(0, count // size)
         def _(step):
-            for r in range(4):
-                t = start + step * 4 + r
+            for r in range(size):
+                t = start + step * size + r
                 for i in range(GROUP):
                     des[dim, i, t] = descent(
                         lambda plane: img[i, plane], vel[i, dim, t + 1], adj[i, t], dim, t
@@ -395,19 +406,21 @@
             )
 
     early_chunks = [(dim, 0, EARLY) for dim in range(3)]
-    late_chunks = [(dim, start, CP) for dim in range(3) for start in range(EARLY, QP, CP)]
+    late_chunks = LATE_CHUNKS
     chunks = early_chunks + late_chunks
     for number, (dim, start, count) in enumerate(late_chunks):
         own_descent(dim, start, count)
         part = (dim, slice(None), pl.ds(start, count))
-        forward(5 + number, des.at[part], lambda way: des_far.at[(way,) + part])
+        forward(7 + number, des.at[part], lambda way: des_far.at[(way,) + part])
     for dim in range(3):
         own_descent(dim, 0, EARLY)
 
     for axis in range(3):
         forwarded(axis, lambda way: vel_far.at[way, :, axis])
-    forwarded(3, lambda way: img_far.at[way])
-    forwarded(4, lambda way: adj_far.at[way])
+    for block in range(2):
+        forwarded(3 + block, image_far(block_planes[block]))
+    forwarded(5, image_far(0))
+    forwarded(6, lambda way: adj_far.at[way])
     for number, (dim, start, count) in enumerate(early_chunks):
         for way in range(2):
             @pl.loop(0, EARLY // 4)
@@ -426,7 +439,7 @@
         smooth(number, dim, start, count)
     for number, (dim, start, count) in enumerate(late_chunks):
         part = (dim, slice(None), pl.ds(start, count))
-        forwarded(5 + number, lambda way: des_far.at[(way,) + part])
+        forwarded(7 + number, lambda way: des_far.at[(way,) + part])
         smooth(len(early_chunks) + number, dim, start, count)
 
     for j in range(GROUP):
@@ -450,9 +463,9 @@
         vmem = lambda *lead: pltpu.VMEM(lead + (XW, YW), f32)
         dma = pltpu.SemaphoreType.DMA
         planes = image.shape[1]
-        late_chunks = 3 * (QP - EARLY) // CP
+        late_chunks = len(LATE_CHUNKS)
         chunks = 3 + late_chunks
-        fields = 5 + QP // PIECE
+        fields = 6 + QP // PIECE
         anywhere = pl.BlockSpec(memory_space=pl.ANY)
         return pl.pallas_call(
             functools.partial(kernel, phases, slabs),
@@ -487,8 +500,8 @@
                 dma((STEPS,)),
                 dma((GROUP,)),
                 dma((GROUP,)),
-                dma((2, 5 + late_chunks)),
-                dma((2, 5 + late_chunks)),
+                dma((2, 7 + late_chunks)),
+                dma((2, 7 + late_chunks)),
                 dma((chunks, GROUP)),
                 dma((chunks, GROUP)),
             ],

time: 93.5 us -> 87 us (0.930)
  Pallas kernels: 90.9 us -> 83.6 us
    pallas_call x1, Pallas kernels: 90.9 us -> 83.6 us  [local(): pl.pallas_call(functools.partial(kernel, phases, slabs), out_shape=(jax.S...]
where the time goes in v4:
time: 87 us; the launch traced here: 86.1 us
  Pallas kernels  83.6 us (96%)
  local copies, waits for them, and re-layouts  1.94 us (2%)
    pallas_call x1, Pallas kernels, local(): pl.pallas_call(functools.partial(kernel, phases, slabs), out_shape=(jax.S...  83.6 us
    unnamed x2, local copies, waits for them, and re-layouts  1.94 us

profile of v4, /device:TPU:1, one launch (start us, length us, event | category | flops | bytes accessed | tf_op | source)
XLA Modules:
  0.0 86.1 jit_solution(15570701458715685927)
XLA Ops:
  0.6 83.6 %shard_map.50 = (f32[1,64,16,128]{3,2,1,0:T(8,128)S(1)}, f32[1,3,64,16,128]{4,3,2,1,0:T(8,128)S(1)}) custom-call(f32[1,3,64,16,128]{4,3,2,1,0:T(8,128)} %v_ref.1, f32[1,64,16,128]{3,2,1,0:T(8,128)} %img_ref.1, f32[1,64,16,128]{3,2,1,0:T(8,128)} %tgt_ref.1), custom_call_target="tpu_custom_call" | custom-call | tf_op jit(solution)/shard_map/pallas_call | solution.py:470
  84.2 0.8 copy.7
  85.0 1.1 %copy.8 = f32[1,3,64,16,128]{4,3,2,1,0:T(8,128)} copy(f32[1,3,64,16,128]{4,3,2,1,0:T(8,128)S(1)} %get-tuple-element.5) | data formatting | bytes 3145728
